TPU v7x, 256 devices: a whole 4x4x8 slice. The times are simulated.
256 devices in a mesh: row: 16 (over y, x), col: 8 (over z_lo, core), band: 2 (over z_hi).
Axes of the slice: x: 4, y: 4, z: 8 (z_hi: 2, z_lo: 4; z = z_hi * 4 + z_lo), core: 2. Of those that a mesh axis runs over, the one named last changes fastest.
Arguments:
- panel: bfloat16 [32, 512, 512], P('row', ('col', 'band')), may hold values from -6 to 6
- inverse: bfloat16 [2, 512, 512], replicated, may hold values from -0.25 to 0.25
- trail_grad: bfloat16 [32, 32, 512, 512], P('row', ('col', 'band')), may hold values from -0.046875 to 0.046875
- factor_grad: bfloat16 [32, 512, 512], P('row', ('col', 'band')), may hold values from -6 to 6
- present: int32 [32, 32], P('row', ('col', 'band')), may hold values from 0 to 1, as said below
- supernode: int32 [32], replicated, may hold values from 0 to 1
Outputs:
- panel_adjoint: bfloat16 [32, 512, 512], P('row', ('col', 'band'))
- inverse_adjoint: float32 [2, 512, 512], replicated
Inputs may be any that keep to these rules, and one draw needn't show every extreme that they name: Every diagonal tile is present; rows differ widely in how many tiles are present.
All inputs are finite; a program needn't handle non-finite values.
Results may differ from a plain program's by a relative error of at most 0.0055.
Values may be sent and summed in bfloat16 or wider, within the bound.
A program may use at most 64 MiB of HBM per device.

v0:
```python
import jax
import jax.numpy as jnp
from jax import lax
from jax.sharding import PartitionSpec as P


def from_root(value, axis, source):
    kept = jnp.where(lax.axis_index(axis) == source, value, 0).astype(value.dtype)
    return lax.psum(kept, axis)


def pick_inverse(inverse, labels):
    first = inverse[0][None, :, :]
    second = inverse[1][None, :, :]
    return jnp.where((labels == 0)[:, None, None], first, second)


def local(panel, inverse, trail_grad, factor_grad, present, supernode):
    rows_here = trail_grad.shape[0]
    cols_here = trail_grad.shape[1]
    tile = trail_grad.shape[2]
    total_rows = rows_here * lax.axis_size("row")
    row_index = lax.axis_index("row")
    col_index = lax.axis_index(("col", "band"))
    row_labels = lax.dynamic_slice_in_dim(supernode, row_index * rows_here, rows_here)
    col_labels = lax.dynamic_slice_in_dim(supernode, col_index * cols_here, cols_here)
    root = col_index * cols_here // rows_here
    row_inverse = pick_inverse(inverse, row_labels)
    factor_piece = jnp.einsum(
        "iab,ibc->iac", panel, row_inverse, preferred_element_type=jnp.float32
    ).astype(jnp.bfloat16)
    factor_row = lax.all_gather(factor_piece, ("col", "band"), axis=1, tiled=True)
    factor_block = from_root(factor_row, "row", root)
    weight = present * (row_labels[:, None] == col_labels[None, :]).astype(jnp.int32)
    masked = trail_grad * weight.astype(jnp.bfloat16)[:, :, None, None]
    mirror_part = jnp.einsum(
        "ijab,iae->jbe", masked, factor_row, preferred_element_type=jnp.float32
    )
    mirror = lax.psum(mirror_part, "row")
    mirror_cols = jnp.transpose(mirror, (1, 0, 2))
    is_owner = (row_index == root).astype(jnp.float32)
    placed = mirror_cols
    placed = placed * is_owner
    direct = jnp.einsum("ijab,jbe->aie", masked, factor_block, preferred_element_type=jnp.float32)
    summed = lax.psum_scatter(direct + placed, ("col", "band"), scatter_dimension=0, tiled=True)
    factor_total = (jnp.transpose(factor_grad.astype(jnp.float32), (1, 0, 2)) - summed).astype(
        jnp.bfloat16
    )
    panel_adjoint = jnp.einsum(
        "aie,ife->iaf", factor_total, row_inverse, preferred_element_type=jnp.float32
    ).astype(jnp.bfloat16)
    onehot = (row_labels[:, None] == jnp.arange(2, dtype=jnp.int32)[None, :]).astype(jnp.float32)
    terms = jnp.einsum("iaf,aie->ife", panel, factor_total, preferred_element_type=jnp.float32)
    local_grad = jnp.einsum("is,ife->sfe", onehot, terms)
    inverse_adjoint = lax.psum(local_grad, ("row", "col", "band")) / jnp.sqrt(
        jnp.float32(total_rows * tile)
    )
    return (panel_adjoint, inverse_adjoint)


def solution(mesh):
    in_specs = (
        P("row", ("col", "band"), None),
        P(),
        P("row", ("col", "band"), None, None),
        P("row", ("col", "band"), None),
        P("row", ("col", "band")),
        P(),
    )
    out_specs = (P("row", ("col", "band"), None), P())
    return jax.shard_map(local, mesh=mesh, in_specs=in_specs, out_specs=out_specs, check_vma=False)
```

profile of v0, /device:TPU:2, one launch (start us, length us, event | category | flops | bytes accessed | tf_op | source)
XLA Modules:
  0.0 711.1 jit_solution(867655354191725240)
XLA Ops:
  7.2 0.0 all-gather.2.cloned.1.call-start
  7.2 1.3 slice_bitcast_fusion.1
  8.5 0.1 broadcast_compare_fusion
  8.6 1.1 fusion.19
  9.7 0.0 all-gather.2.cloned.1.call-update
  9.7 0.0 all-reduce.6.cloned.1.call-start
  9.8 92.1 %all-gather.2.cloned.1.call-done = bf16[2,512,512]{2,1,0:T(8,128)(2,1)} async-done(((bf16[2,32,512]{2,1,0:T(8,128)(2,1)}), bf16[2,512,512]{2,1,0:T(8,128)(2,1)}) %all-gather.2.cloned.1.call-update) | async-done | bytes 1048592 | tf_op jit(solution)/shard_map/all_gather | solution.py:32
  101.9 1.1 broadcast_select_fusion
  103.0 0.0 all-reduce.8.cloned.1.call-start
  103.1 0.1 dynamic_slice.7
  103.2 0.1 fusion.36
  103.2 0.3 copy-done.1
  103.5 4.2 fusion.4
  107.8 0.0 all-reduce.8.cloned.1.call-update
  107.8 0.0 all-reduce.12.cloned.1.call-start
  107.8 96.2 %all-reduce.6.cloned.1.call-done = bf16[2,512,512]{2,1,0:T(8,128)(2,1)} async-done(((bf16[2,512,512]{2,1,0:T(8,128)(2,1)}), bf16[2,512,512]{2,1,0:T(8,128)(2,1)}) %all-reduce.6.cloned.1.call-update) | async-done | bytes 1048592 | tf_op jit(solution)/shard_map/psum | solution.py:9
  204.0 104.7 %all-reduce.8.cloned.1.call-done = f32[2,512,512]{1,2,0:T(8,128)} async-done(((f32[2,512,512]{1,2,0:T(8,128)}), f32[2,512,512]{1,2,0:T(8,128)}) %all-reduce.8.cloned.1.call-update) | async-done | bytes 2097168 | tf_op jit(solution)/shard_map/psum | solution.py:39
  308.8 3.9 bitcast_add_fusion
  312.7 2.4 copy.26
  315.1 0.0 all-reduce.12.cloned.1.call-update
  315.1 0.0 all-reduce.10.cloned.1.call-start
  315.2 0.6 copy-done.5
  315.8 0.6 dynamic-slice
  317.0 113.6 %all-reduce.12.cloned.1.call-done = f32[512,2,512]{2,1,0:T(2,128)} async-done(((f32[512,2,512]{2,1,0:T(2,128)}), f32[512,2,512]{2,1,0:T(2,128)}) %all-reduce.12.cloned.1.call-update) | async-done | bytes 2097168
  430.6 0.9 constant_dynamic-slice_fusion
  431.6 0.5 convolution_bitcast_fusion
  432.1 1.0 copy.29
  433.1 2.8 fusion.33
  435.9 1.1 fusion.16
  437.0 263.4 %all-reduce.10.cloned.1.call-done = f32[2,512,512]{2,0,1:T(2,128)} async-done(((f32[2,512,512]{2,0,1:T(2,128)}), f32[2,512,512]{2,0,1:T(2,128)}) %all-reduce.10.cloned.1.call-update) | async-done | bytes 2097168 | tf_op jit(solution)/shard_map/psum | solution.py:55
  700.4 2.5 broadcast_multiply_fusion
  702.9 1.7 copy.30
  (12 shorter events, 0.1 us)
Async XLA Ops:
  7.2 1.4 copy-start
  7.2 1.3 copy-start.4
  7.2 94.7 %all-gather.2.cloned.1.call-start = ((), (), s32[]{:S(2)}) async-start(), calls=%async_computation | async-start | bytes 1114112 | tf_op jit(solution)/shard_map/all_gather | solution.py:32
  8.6 94.6 %copy-start.3 = (s32[2,2]{1,0:T(2,128)S(1)}, s32[2,2]{1,0:T(2,128)}, u32[]{:S(2)}) copy-start(s32[2,2]{1,0:T(2,128)} %param.10) | copy-start | bytes 52
  9.7 194.3 %all-reduce.6.cloned.1.call-start = ((), (), s32[]{:S(2)}) async-start(), calls=%async_computation.1 | async-start | bytes 2097152 | tf_op jit(solution)/shard_map/psum | solution.py:9
  101.9 1.6 copy-start.1
  103.0 205.7 %all-reduce.8.cloned.1.call-start = ((), (), s32[]{:S(2)}) async-start(), calls=%async_computation.2 | async-start | bytes 4194304 | tf_op jit(solution)/shard_map/psum | solution.py:39
  107.8 322.9 %all-reduce.12.cloned.1.call-start = ((), (), s32[]{:S(2)}) async-start(), calls=%async_computation.4 | async-start | bytes 4194304
  315.1 0.7 copy-start.5
  315.1 116.5 %copy-start.2 = (bf16[2,32,512]{2,1,0:T(8,128)(2,1)S(1)}, bf16[2,32,512]{2,1,0:T(8,128)(2,1)}, u32[]{:S(2)}) copy-start(bf16[2,32,512]{2,1,0:T(8,128)(2,1)} %param.9) | copy-start | bytes 196612
  315.1 385.3 %all-reduce.10.cloned.1.call-start = ((), (), s32[]{:S(2)}) async-start(), calls=%async_computation.3 | async-start | bytes 4194304 | tf_op jit(solution)/shard_map/psum | solution.py:55
Sparse Core Ops, SparseCore 0:
  10.4 91.5 all-gather.1
  105.2 98.8 all-reduce.5
  207.9 100.7 all-reduce.7
  315.3 115.3 all-reduce.11
  436.4 263.9 all-reduce.9
where the time goes:
time: 711 us
  waiting for transfers between devices  670 us (94%)
  between operations  14.5 us (2%)
  matrix products  13.7 us (2%)
  local copies, waits for them, and re-layouts  8.87 us (1%)
    psum x1, waiting for transfers between devices, local(): lax.psum(local_grad, ('row', 'col', 'band'))  263 us
    unnamed x6, waiting for transfers between devices  114 us
    psum x1, waiting for transfers between devices, local(): mirror = lax.psum(mirror_part, 'row')  105 us
    psum x1, waiting for transfers between devices, from_root(): return lax.psum(kept, axis)  96.2 us
    all_gather x1, waiting for transfers between devices, local(): lax.all_gather(factor_piece, ('col', 'band'), axis=1, tiled=True)  92.1 us
  transfers between devices with their start and end apart: 5, of which 5 were waited for; matrix products, arithmetic and copies ran while one was open for 1% of the time, Pallas kernels for 0%

commit v1 on v0

--- a/solution.py
+++ b/solution.py
@@ -36,7 +36,7 @@
     mirror_part = jnp.einsum(
         "ijab,iae->jbe", masked, factor_row, preferred_element_type=jnp.float32
     )
-    mirror = lax.psum(mirror_part, "row")
+    mirror = jnp.sum(lax.all_gather(mirror_part, "row"), axis=0)
     mirror_cols = jnp.transpose(mirror, (1, 0, 2))
     is_owner = (row_index == root).astype(jnp.float32)
     placed = mirror_cols

time: 711 us -> 813 us (1.14)
  waiting for transfers between devices: 670 us -> 756 us
  other arithmetic: 3.72 us -> 16.5 us
    all_gather x0 -> x1, waiting for transfers between devices: none -> 202 us  [local(): mirror = jnp.sum(lax.all_gather(mirror_part, 'row'), axis=0)]
    psum x1 -> x0, waiting for transfers between devices: 105 us -> none  [local(): mirror = lax.psum(mirror_part, 'row')]
    reduce_sum x0 -> x1, other arithmetic: none -> 12.7 us  [local(): mirror = jnp.sum(lax.all_gather(mirror_part, 'row'), axis=0)]
    psum x1, waiting for transfers between devices: 96.2 us -> 85.4 us  [from_root(): return lax.psum(kept, axis)]
  transfers between devices with their start and end apart: 5 -> 5, of which waited for: 5 -> 5; matrix products, arithmetic and copies ran while one was open for 1% -> 2% of each run, Pallas kernels for 0% -> 0%
where the time goes in v1:
time: 813 us; the launch traced here: 812 us
  waiting for transfers between devices  756 us (93%)
  other arithmetic  16.5 us (2%)
  between operations  14.6 us (2%)
  matrix products  13.3 us (2%)
  local copies, waits for them, and re-layouts  11.7 us (1%)
    psum x1, waiting for transfers between devices, local(): lax.psum(local_grad, ('row', 'col', 'band'))  263 us
    all_gather x1, waiting for transfers between devices, local(): mirror = jnp.sum(lax.all_gather(mirror_part, 'row'), axis=0)  202 us
    unnamed x6, waiting for transfers between devices  114 us
    all_gather x1, waiting for transfers between devices, local(): lax.all_gather(factor_piece, ('col', 'band'), axis=1, tiled=True)  91.9 us
    psum x1, waiting for transfers between devices, from_root(): return lax.psum(kept, axis)  85.4 us
  transfers between devices with their start and end apart: 5, of which 5 were waited for; matrix products, arithmetic and copies ran while one was open for 2% of the time, Pallas kernels for 0%

profile of v1, /device:TPU:2, one launch (start us, length us, event | category | flops | bytes accessed | tf_op | source)
XLA Modules:
  0.0 812.4 jit_solution(15020717351046019355)
XLA Ops:
  7.2 0.0 all-gather.4.cloned.1.call-start
  7.3 1.4 slice_bitcast_fusion.1
  8.7 0.1 broadcast_compare_fusion
  8.8 1.1 fusion.19
  9.9 0.0 all-gather.6.cloned.1.call-start
  9.9 0.1 dynamic_slice.7
  10.0 0.1 fusion.36
  10.1 91.9 %all-gather.4.cloned.1.call-done = bf16[2,512,512]{2,1,0:T(8,128)(2,1)} async-done(((bf16[2,32,512]{2,1,0:T(8,128)(2,1)}), bf16[2,512,512]{2,1,0:T(8,128)(2,1)}) %all-gather.4.cloned.1.call-update) | async-done | bytes 1048592 | tf_op jit(solution)/shard_map/all_gather | solution.py:32
  102.0 3.9 fusion.4
  105.8 0.0 all-gather.6.cloned.1.call-update
  105.9 0.0 all-reduce.5.cloned.1.call-start
  105.9 1.1 copy-done.1
  107.1 1.1 broadcast_select_fusion
  108.2 0.0 all-reduce.9.cloned.1.call-start
  108.2 201.7 %all-gather.6.cloned.1.call-done = f32[32,512,512]{2,1,0:T(8,128)} async-done(((f32[2,512,512]{2,1,0:T(8,128)}), f32[32,512,512]{2,1,0:T(8,128)}) %all-gather.6.cloned.1.call-update) | async-done | bytes 33554448 | tf_op jit(solution)/shard_map/all_gather | solution.py:39
  309.9 12.7 %reduce_sum.9 = f32[2,512,512]{2,1,0:T(8,128)S(1)} reduce(f32[16,2,512,512]{3,2,1,0:T(8,128)} %bitcast.39, f32[]{:T(128)} %constant.38.clone.1), dimensions={0}, to_apply=%region_1.2 | reduce | flops 7864320 | bytes 35651588 | tf_op jit(solution)/shard_map/reduce_sum | solution.py:39
  322.7 1.8 copy.24
  324.5 85.4 %all-reduce.5.cloned.1.call-done = bf16[2,512,512]{2,1,0:T(8,128)(2,1)} async-done(((bf16[2,512,512]{2,1,0:T(8,128)(2,1)}), bf16[2,512,512]{2,1,0:T(8,128)(2,1)}) %all-reduce.5.cloned.1.call-update) | async-done | bytes 1048592 | tf_op jit(solution)/shard_map/psum | solution.py:9
  409.9 3.9 bitcast_add_fusion
  413.8 2.4 copy.25
  416.3 0.0 all-reduce.7.cloned.1.call-start
  416.3 0.6 copy-done.6
  416.9 0.6 dynamic-slice
  418.2 113.8 %all-reduce.9.cloned.1.call-done = f32[512,2,512]{2,1,0:T(2,128)} async-done(((f32[512,2,512]{2,1,0:T(2,128)}), f32[512,2,512]{2,1,0:T(2,128)}) %all-reduce.9.cloned.1.call-update) | async-done | bytes 2097168
  532.0 0.9 constant_dynamic-slice_fusion
  532.9 0.5 convolution_bitcast_fusion
  533.4 1.0 copy.28
  534.4 2.8 fusion.33
  537.2 1.1 fusion.16
  538.4 263.4 %all-reduce.7.cloned.1.call-done = f32[2,512,512]{2,0,1:T(2,128)} async-done(((f32[2,512,512]{2,0,1:T(2,128)}), f32[2,512,512]{2,0,1:T(2,128)}) %all-reduce.7.cloned.1.call-update) | async-done | bytes 2097168 | tf_op jit(solution)/shard_map/psum | solution.py:55
  801.7 2.5 broadcast_multiply_fusion
  804.2 1.7 copy.29
  (16 shorter events, 0.1 us)
Async XLA Ops:
  7.2 1.6 copy-start
  7.2 1.5 copy-start.4
  7.2 2.8 copy-start.3
  7.2 94.8 %copy-start.5 = (bf16[2,2,512,512]{3,2,1,0:T(8,128)(2,1)S(1)}, bf16[2,2,512,512]{3,2,1,0:T(8,128)(2,1)}, u32[]{:S(2)}) copy-start(bf16[2,2,512,512]{3,2,1,0:T(8,128)(2,1)} %param.8) | copy-start | bytes 6291460
  7.2 94.7 %all-gather.4.cloned.1.call-start = ((), (), s32[]{:S(2)}) async-start(), calls=%async_computation | async-start | bytes 1114112 | tf_op jit(solution)/shard_map/all_gather | solution.py:32
  9.9 300.1 %all-gather.6.cloned.1.call-start = ((), (), s32[]{:S(2)}) async-start(), calls=%async_computation.3 | async-start | bytes 35651584 | tf_op jit(solution)/shard_map/all_gather | solution.py:39
  105.8 1.2 copy-start.1
  105.9 304.0 %all-reduce.5.cloned.1.call-start = ((), (), s32[]{:S(2)}) async-start(), calls=%async_computation.1 | async-start | bytes 2097152 | tf_op jit(solution)/shard_map/psum | solution.py:9
  108.2 423.8 %all-reduce.9.cloned.1.call-start = ((), (), s32[]{:S(2)}) async-start(), calls=%async_computation.4 | async-start | bytes 4194304
  416.3 0.7 copy-start.6
  416.3 116.6 %copy-start.2 = (bf16[2,32,512]{2,1,0:T(8,128)(2,1)S(1)}, bf16[2,32,512]{2,1,0:T(8,128)(2,1)}, u32[]{:S(2)}) copy-start(bf16[2,32,512]{2,1,0:T(8,128)(2,1)} %param.9) | copy-start | bytes 196612
  416.3 385.4 %all-reduce.7.cloned.1.call-start = ((), (), s32[]{:S(2)}) async-start(), calls=%async_computation.2 | async-start | bytes 4194304 | tf_op jit(solution)/shard_map/psum | solution.py:55
Sparse Core Ops, SparseCore 0:
  10.4 91.5 all-gather.3
  106.0 203.9 all-gather.5
  313.2 96.6 all-reduce.4
  416.4 115.5 all-reduce.8
  537.8 263.9 all-reduce.6

commit v2 on v0

--- a/solution.py
+++ b/solution.py
@@ -29,7 +29,12 @@
     factor_piece = jnp.einsum(
         "iab,ibc->iac", panel, row_inverse, preferred_element_type=jnp.float32
     ).astype(jnp.bfloat16)
-    factor_row = lax.all_gather(factor_piece, ("col", "band"), axis=1, tiled=True)
+    factor_row = jnp.concatenate(
+        lax.all_to_all(
+            jnp.stack([factor_piece] * lax.axis_size(("col", "band"))), ("col", "band"), 0, 0
+        ),
+        axis=1,
+    )
     factor_block = from_root(factor_row, "row", root)
     weight = present * (row_labels[:, None] == col_labels[None, :]).astype(jnp.int32)
     masked = trail_grad * weight.astype(jnp.bfloat16)[:, :, None, None]

time: 711 us -> 651 us (0.916)
  waiting for transfers between devices: 670 us -> 600 us
  starting transfers between devices: 0.21 us -> 8.74 us
    all_gather x1 -> x0, waiting for transfers between devices: 92.1 us -> none  [local(): lax.all_gather(factor_piece, ('col', 'band'), axis=1, tiled=True)]
    all_to_all x0 -> x1, waiting for transfers between devices: none -> 28.8 us  [local(): lax.all_to_all(jnp.stack([factor_piece] * lax.axis_size(('col', 'band')))...]
    all_to_all x0 -> x1, starting transfers between devices: none -> 8.57 us  [local(): lax.all_to_all(jnp.stack([factor_piece] * lax.axis_size(('col', 'band')))...]
    unnamed x6 -> x5, waiting for transfers between devices: 114 us -> 114 us
where the time goes in v2:
time: 651 us; the launch traced here: 650 us
  waiting for transfers between devices  600 us (92%)
  between operations  14.6 us (2%)
  matrix products  13 us (2%)
  local copies, waits for them, and re-layouts  10.3 us (2%)
  starting transfers between devices  8.74 us (1%)
    psum x1, waiting for transfers between devices, local(): lax.psum(local_grad, ('row', 'col', 'band'))  263 us
    unnamed x5, waiting for transfers between devices  114 us
    psum x1, waiting for transfers between devices, local(): mirror = lax.psum(mirror_part, 'row')  105 us
    psum x1, waiting for transfers between devices, from_root(): return lax.psum(kept, axis)  89.5 us
    all_to_all x1, waiting for transfers between devices, local(): lax.all_to_all(jnp.stack([factor_piece] * lax.axis_size(('col', 'band')))...  28.8 us
  transfers between devices with their start and end apart: 5, of which 5 were waited for; matrix products, arithmetic and copies ran while one was open for 1% of the time, Pallas kernels for 0%

profile of v2, /device:TPU:2, one launch (start us, length us, event | category | flops | bytes accessed | tf_op | source)
XLA Modules:
  0.0 650.5 jit_solution(14550433136138831093)
XLA Ops:
  7.2 1.3 slice_bitcast_fusion.1
  8.5 0.1 broadcast_compare_fusion
  8.6 0.4 fusion.19
  9.0 1.1 stack.2
  10.1 8.6 %all-to-all-start = ((bf16[16,2,32,512]{3,2,1,0:T(8,128)(2,1)}), bf16[16,2,32,512]{3,2,1,0:T(8,128)(2,1)S(1)}, u32[]{:S(2)}, u32[]{:S(2)}) async-start(bf16[16,2,32,512]{3,2,1,0:T(8,128)(2,1)} %stack.2), calls=%async_computation | async-start | bytes 2097152 | tf_op jit(solution)/shard_map/all_to_all | solution.py:33
  18.7 0.0 all-reduce.6.cloned.1.call-start
  18.8 28.8 %all-to-all-done = bf16[16,2,32,512]{3,2,1,0:T(8,128)(2,1)S(1)} async-done(((bf16[16,2,32,512]{3,2,1,0:T(8,128)(2,1)}), bf16[16,2,32,512]{3,2,1,0:T(8,128)(2,1)S(1)}, u32[]{:S(2)}, u32[]{:S(2)}) %all-to-all-start) | async-done | bytes 1048608 | tf_op jit(solution)/shard_map/all_to_all | solution.py:33
  47.6 0.1 copy.34
  47.7 0.5 copy.35
  48.3 1.1 broadcast_select_fusion
  49.3 0.0 all-reduce.6.cloned.1.call-update
  49.3 0.0 all-reduce.8.cloned.1.call-start
  49.4 0.1 dynamic_slice.7
  49.5 0.1 fusion.35
  49.6 4.2 fusion.4
  53.8 0.0 all-reduce.12.cloned.1.call-start
  53.9 89.5 %all-reduce.6.cloned.1.call-done = bf16[2,512,512]{1,2,0:T(8,128)(2,1)} async-done(((bf16[2,512,512]{1,2,0:T(8,128)(2,1)}), bf16[2,512,512]{1,2,0:T(8,128)(2,1)}) %all-reduce.6.cloned.1.call-update) | async-done | bytes 1048592 | tf_op jit(solution)/shard_map/psum | solution.py:9
  143.4 104.7 %all-reduce.8.cloned.1.call-done = f32[2,512,512]{1,2,0:T(8,128)} async-done(((f32[2,512,512]{1,2,0:T(8,128)}), f32[2,512,512]{1,2,0:T(8,128)}) %all-reduce.8.cloned.1.call-update) | async-done | bytes 2097168 | tf_op jit(solution)/shard_map/psum | solution.py:44
  248.1 3.9 bitcast_add_fusion
  252.0 2.4 copy.38
  254.4 0.0 all-reduce.10.cloned.1.call-start
  254.5 0.6 copy-done.4
  255.1 0.6 dynamic-slice
  256.3 113.6 %all-reduce.12.cloned.1.call-done = f32[512,2,512]{2,1,0:T(2,128)} async-done(((f32[512,2,512]{2,1,0:T(2,128)}), f32[512,2,512]{2,1,0:T(2,128)}) %all-reduce.12.cloned.1.call-update) | async-done | bytes 2097168
  370.0 0.9 constant_dynamic-slice_fusion
  370.9 0.5 convolution_bitcast_fusion
  371.4 1.0 copy.41
  372.4 2.8 fusion.32
  375.2 1.1 fusion.16
  376.3 263.4 %all-reduce.10.cloned.1.call-done = f32[2,512,512]{2,0,1:T(2,128)} async-done(((f32[2,512,512]{2,0,1:T(2,128)}), f32[2,512,512]{2,0,1:T(2,128)}) %all-reduce.10.cloned.1.call-update) | async-done | bytes 2097168 | tf_op jit(solution)/shard_map/psum | solution.py:60
  639.7 2.5 broadcast_multiply_fusion
  642.2 1.7 copy.42
  (12 shorter events, 0.1 us)
Async XLA Ops:
  7.2 1.4 copy-start
  7.2 1.3 copy-start.3
  10.1 37.4 %all-to-all-start = ((bf16[16,2,32,512]{3,2,1,0:T(8,128)(2,1)}), bf16[16,2,32,512]{3,2,1,0:T(8,128)(2,1)S(1)}, u32[]{:S(2)}, u32[]{:S(2)}) async-start(bf16[16,2,32,512]{3,2,1,0:T(8,128)(2,1)} %stack.2), calls=%async_computation | async-start | bytes 2097152 | tf_op jit(solution)/shard_map/all_to_all | solution.py:33
  18.7 124.7 %all-reduce.6.cloned.1.call-start = ((), (), s32[]{:S(2)}) async-start(), calls=%async_computation.1 | async-start | bytes 2097152 | tf_op jit(solution)/shard_map/psum | solution.py:9
  48.2 1.2 copy-start.2
  49.3 198.7 %all-reduce.8.cloned.1.call-start = ((), (), s32[]{:S(2)}) async-start(), calls=%async_computation.2 | async-start | bytes 4194304 | tf_op jit(solution)/shard_map/psum | solution.py:44
  53.8 316.2 %all-reduce.12.cloned.1.call-start = ((), (), s32[]{:S(2)}) async-start(), calls=%async_computation.4 | async-start | bytes 4194304
  254.4 0.7 copy-start.4
  254.4 116.5 %copy-start.1 = (bf16[2,32,512]{2,1,0:T(8,128)(2,1)S(1)}, bf16[2,32,512]{2,1,0:T(8,128)(2,1)}, u32[]{:S(2)}) copy-start(bf16[2,32,512]{2,1,0:T(8,128)(2,1)} %param.9) | copy-start | bytes 196612
  254.4 385.3 %all-reduce.10.cloned.1.call-start = ((), (), s32[]{:S(2)}) async-start(), calls=%async_computation.3 | async-start | bytes 4194304 | tf_op jit(solution)/shard_map/psum | solution.py:60
Sparse Core Ops, SparseCore 0:
  49.5 93.8 all-reduce.5
  147.3 100.7 all-reduce.7
  254.6 115.3 all-reduce.11
  375.8 263.9 all-reduce.9
